TPU v7x, 32 devices: a whole 2x2x4 slice. The times are simulated.
32 devices in a mesh: blk: 8 (over z, y), ch: 4 (over x, core).
Axes of the slice: x: 2, y: 2, z: 4, core: 2. Of those that a mesh axis runs over, the one named last changes fastest.
Arguments:
- features: bfloat16 [6144, 512], P('blk', 'ch'), may hold values from -6 to 6
- tile_values: bfloat16 [1024, 128, 128], P('blk'), may hold values from -600 to 600
- tile_source: int32 [1024], P('blk'), may hold values from 0 to 48, as said below
- tile_target: int32 [1024], P('blk'), may hold values from 0 to 5
- tile_count: int32 [8], P('blk'), may hold values from 32 to 128
- weights: bfloat16 [3, 512, 512], replicated, may hold values from -0.15625 to 0.15625
- bias_vector: float32 [512], replicated, may hold values from -3 to 3
Outputs:
- mixed: bfloat16 [6144, 512], P('blk', 'ch')
Inputs may be any that keep to these rules, and one draw needn't show every extreme that they name: `tile_source`: in each index of blk the live slots come first, sorted by value, and at most 32 of them name row tiles of one index of blk (tiles 6 * b to 6 * b + 5), a bound that every index of blk reaches; slots from tile_count on hold 48.
All inputs are finite; a program needn't handle non-finite values.
Results may differ from a plain program's by a relative error of at most 0.01.
Values may be sent and summed in bfloat16 or wider, within the bound.
A program may use at most 64 MiB of HBM per device.

v0:
```python
import jax
import jax.numpy as jnp
from jax import lax
from jax.sharding import PartitionSpec as P


def per_device(features, tile_values, tile_source, tile_target, tile_count, weights, bias_vector):
    tile_size = tile_values.shape[1]
    slot_total = tile_values.shape[0]
    channels = features.shape[1]
    row_tiles = features.shape[0] // tile_size
    block_rows = row_tiles * tile_size
    block_count = lax.axis_size("blk")
    slot_cap = max(2, (2 * slot_total + block_count - 1) // block_count)
    usable = jnp.arange(slot_total, dtype=jnp.int32) < tile_count[0]
    squares = jnp.einsum(
        "tij,tij->ti", tile_values, tile_values, preferred_element_type=jnp.float32
    )
    squares = jnp.where(usable[:, None], squares, 0.0)
    onehot = (
        (tile_target[:, None] == jnp.arange(row_tiles, dtype=jnp.int32)[None, :]) & usable[:, None]
    ).astype(jnp.float32)
    row_norm = jnp.dot(onehot.T, squares, precision=lax.Precision.HIGHEST)
    inverse = lax.rsqrt(1.0 + row_norm).reshape(-1)
    zero_sum = jnp.zeros((row_tiles, tile_size, channels), jnp.float32)

    def cycle_prop(signal):
        segment = lax.all_gather(signal, "blk", axis=0, tiled=True)
        offset = jnp.int32(0)
        count_rows = segment.shape[0]
        window = min(slot_total, slot_cap * (count_rows // block_rows + 2))
        low_row = tile_source * tile_size
        first_slot = jnp.sum(usable & (low_row + tile_size <= offset))
        end_slot = jnp.sum(usable & (low_row < offset + count_rows))
        start_slot = jnp.minimum(first_slot, slot_total - window)
        slot_ids = start_slot + jnp.arange(window, dtype=jnp.int32)
        in_range = (slot_ids >= first_slot) & (slot_ids < end_slot)
        row_ids = tile_source[:, None] * tile_size + jnp.arange(tile_size, dtype=jnp.int32)[None, :]
        inside = (row_ids >= 0) & (row_ids < count_rows) & in_range[:, None]
        picked = jnp.take(segment, jnp.clip(row_ids, 0, count_rows - 1).reshape(-1), axis=0)
        picked = picked.reshape(window, tile_size, channels)
        picked = jnp.where(inside[:, :, None], picked, jnp.zeros((), segment.dtype))
        product = jnp.einsum(
            "gij,gjc->gic", tile_values, picked, preferred_element_type=jnp.float32
        )
        product = jnp.where(in_range[:, None, None], product, 0.0)
        summed = zero_sum.at[tile_target].add(product)
        return summed.reshape(-1, channels) * inverse[:, None]

    col_start = lax.axis_index("ch") * channels
    bias_part = lax.dynamic_slice_in_dim(bias_vector, col_start, channels, 0)
    w_cols = lax.dynamic_slice_in_dim(weights, col_start, channels, 2)

    def mix_term(order_term, order_index, running):
        w_slice = w_cols[order_index]
        return running + jnp.dot(
            lax.all_gather(order_term, "ch", axis=1, tiled=True),
            w_slice,
            preferred_element_type=jnp.float32,
        )

    result = mix_term(features, 0, jnp.zeros((features.shape[0], channels), jnp.float32))
    first_order = cycle_prop(features).astype(jnp.bfloat16)
    result = mix_term(first_order, 1, result)
    second_order = (2.0 * cycle_prop(first_order) - features.astype(jnp.float32)).astype(
        jnp.bfloat16
    )
    result = mix_term(second_order, 2, result)
    return (result + bias_part[None, :]).astype(jnp.bfloat16)


def solution(mesh):
    return jax.shard_map(
        per_device,
        mesh=mesh,
        in_specs=(P("blk", "ch"), P("blk", None, None), P("blk"), P("blk"), P("blk"), P(), P()),
        out_specs=P("blk", "ch"),
        check_vma=False,
    )
```

profile of v0, /device:TPU:0, one launch (start us, length us, event | category | flops | bytes accessed | tf_op | source)
XLA Modules:
  0.0 337.5 jit_solution(6687405076137406024)
XLA Ops:
  6.5 0.0 copy-start
  6.5 0.0 copy-start.2
  6.5 0.0 all-gather.3.cloned.1.call-start
  6.5 0.7 all-gather.3.cloned.1.call-update
  7.3 0.0 all-gather.5.cloned.1.call-start
  8.0 1.4 fusion.43
  10.1 1.3 compare_and_fusion
  11.3 4.4 %fusion = f32[128,128]{1,0:T(8,128)S(1)} fusion(bf16[128,128,128]{2,1,0:T(8,128)(2,1)} %param.10), kind=kLoop, calls=%fused_computation.5 | loop fusion | flops 6275072 | bytes 4259840 | tf_op jit(solution)/shard_map/tij,tij->ti/dot_general | solution.py:16
  15.7 0.0 copy-done.2
  15.8 0.3 fusion.18
  16.0 0.1 fusion.33
  16.2 0.1 fusion.31
  16.3 0.1 fusion.28
  16.4 40.1 %all-gather.3.cloned.1.call-done = bf16[6144,128]{1,0:T(8,128)(2,1)} async-done(((bf16[768,128]{1,0:T(8,128)(2,1)}), bf16[6144,128]{1,0:T(8,128)(2,1)}) %all-gather.3.cloned.1.call-update) | async-done | bytes 1572880 | tf_op jit(solution)/shard_map/all_gather | solution.py:28
  56.5 56.5 %gather_fusion = bf16[16384,128]{1,0:T(8,128)(2,1)} fusion(bf16[6144,128]{1,0:T(8,128)(2,1)} %all-gather.3.cloned.1.call-done, s32[16384]{0:T(1024)S(1)} %fusion.28), kind=kCustom, calls=%fused_computation.clone | custom fusion | bytes 8454144 | tf_op jit(solution)/shard_map/jit(_take)/gather | solution.py:40
  112.9 11.5 %broadcast_select_fusion.1 = bf16[16384,128]{1,0:T(8,128)(2,1)} fusion(bf16[16384,128]{1,0:T(8,128)(2,1)} %gather_fusion, pred[16384]{0:T(1024)(128)(4,1)S(1)} %fusion.31), kind=kLoop, calls=%fused_computation.13 | loop fusion | flops 2097152 | bytes 8404992 | tf_op jit(solution)/shard_map/jit(_take)/select_n | solution.py:40
  124.4 6.3 %copy.8 = bf16[128,128,128]{1,2,0:T(8,128)(2,1)} copy(bf16[128,128,128]{2,1,0:T(8,128)(2,1)} %bitcast.60) | data formatting | bytes 8388608 | tf_op jit(solution)/shard_map/reshape | solution.py:41
  130.8 9.7 %select_bitcast_fusion.1 = f32[128,128,128]{1,2,0:T(8,128)} fusion(pred[128]{0:T(512)(128)(4,1)S(1)} %compare_and_fusion, bf16[128,128,128]{2,1,0:T(8,128)(2,1)} %param.10, bf16[128,128,128]{1,2,0:T(8,128)(2,1)} %copy.8, pred[128,128]{1,0:T(8,128)(4,1)S(1)} %fusion.33), kind=kOutput, calls=%fused_computation.7 | convolution fusion | flops 541065216 | bytes 16793728 | tf_op jit(solution)/shard_map/gij,gjc->gic/dot_general | solution.py:43
  140.5 9.0 %copy.9 = f32[128,128,128]{2,1,0:T(8,128)} copy(f32[128,128,128]{1,2,0:T(8,128)} %select_bitcast_fusion.1) | data formatting | bytes 16777216 | tf_op jit(solution)/shard_map/jit(_where)/select_n | solution.py:46
  149.5 0.0 copy-start.1
  149.6 17.0 %scatter_fusion = f32[6,128,128]{2,1,0:T(8,128)S(1)} fusion(f32[6,128,128]{2,1,0:T(8,128)S(1)} %broadcast_in_dim.75.clone, s32[128]{0:T(128)S(1)} %get-tuple-element.9, f32[128,128,128]{2,1,0:T(8,128)} %copy.9), kind=kCustom, calls=%fused_computation.2 | custom fusion | flops 2097152 | bytes 25166336 | tf_op jit(solution)/shard_map/scatter-add | solution.py:47
  166.6 0.8 fusion.22
  167.4 0.0 all-gather.5.cloned.1.call-update
  167.5 0.8 dynamic_slice.7
  168.2 0.0 copy-done.1
  168.2 8.6 %all_gather.15 = bf16[768,512]{1,0:T(8,128)(2,1)S(1)} all-gather(bf16[768,128]{1,0:T(8,128)(2,1)S(1)} %copy-done.1), channel_id=1, replica_groups=mesh['blk'=8,'ch'=4] {'ch'}, dimensions={1}, use_global_device_ids=true | all-gather | bytes 983040 | tf_op jit(solution)/shard_map/all_gather | solution.py:57
  176.8 9.1 %all_gather.17 = bf16[768,512]{1,0:T(8,128)(2,1)S(1)} all-gather(bf16[768,128]{1,0:T(8,128)(2,1)} %fusion.22), channel_id=1, replica_groups=mesh['blk'=8,'ch'=4] {'ch'}, dimensions={1}, use_global_device_ids=true | all-gather | bytes 983040 | tf_op jit(solution)/shard_map/all_gather | solution.py:57
  185.9 0.0 copy-done
  185.9 0.4 fusion.24
  186.3 23.9 %all-gather.5.cloned.1.call-done = bf16[6144,128]{1,0:T(8,128)(2,1)} async-done(((bf16[768,128]{1,0:T(8,128)(2,1)}), bf16[6144,128]{1,0:T(8,128)(2,1)}) %all-gather.5.cloned.1.call-update) | async-done | bytes 1572880 | tf_op jit(solution)/shard_map/all_gather | solution.py:28
  210.2 56.5 %gather_fusion.1 = bf16[16384,128]{1,0:T(8,128)(2,1)} fusion(bf16[6144,128]{1,0:T(8,128)(2,1)} %all-gather.5.cloned.1.call-done, s32[16384]{0:T(1024)S(1)} %fusion.28), kind=kCustom, calls=%fused_computation.1.clone | custom fusion | bytes 8454144 | tf_op jit(solution)/shard_map/jit(_take)/gather | solution.py:40
  266.7 11.5 %broadcast_select_fusion = bf16[16384,128]{1,0:T(8,128)(2,1)} fusion(bf16[16384,128]{1,0:T(8,128)(2,1)} %gather_fusion.1, pred[16384]{0:T(1024)(128)(4,1)S(1)} %fusion.31), kind=kLoop, calls=%fused_computation.12 | loop fusion | flops 2097152 | bytes 8404992 | tf_op jit(solution)/shard_map/jit(_take)/select_n | solution.py:40
  278.2 6.3 %copy.11 = bf16[128,128,128]{1,2,0:T(8,128)(2,1)} copy(bf16[128,128,128]{2,1,0:T(8,128)(2,1)} %bitcast.59) | data formatting | bytes 8388608 | tf_op jit(solution)/shard_map/reshape | solution.py:41
  284.5 9.7 %select_bitcast_fusion = f32[128,128,128]{1,2,0:T(8,128)} fusion(pred[128]{0:T(512)(128)(4,1)S(1)} %compare_and_fusion, bf16[128,128,128]{2,1,0:T(8,128)(2,1)} %param.10, bf16[128,128,128]{1,2,0:T(8,128)(2,1)} %copy.11, pred[128,128]{1,0:T(8,128)(4,1)S(1)} %fusion.33), kind=kOutput, calls=%fused_computation.6 | convolution fusion | flops 541065216 | bytes 16793728 | tf_op jit(solution)/shard_map/gij,gjc->gic/dot_general | solution.py:43
  294.2 9.0 %copy.12 = f32[128,128,128]{2,1,0:T(8,128)} copy(f32[128,128,128]{1,2,0:T(8,128)} %select_bitcast_fusion) | data formatting | bytes 16777216 | tf_op jit(solution)/shard_map/jit(_where)/select_n | solution.py:46
  303.3 17.0 %scatter_fusion.1 = f32[6,128,128]{2,1,0:T(8,128)S(1)} fusion(f32[6,128,128]{2,1,0:T(8,128)S(1)} %broadcast_in_dim.75, s32[128]{0:T(128)S(1)} %get-tuple-element.9, f32[128,128,128]{2,1,0:T(8,128)} %copy.12), kind=kCustom, calls=%fused_computation.3 | custom fusion | flops 2097152 | bytes 25166336 | tf_op jit(solution)/shard_map/scatter-add | solution.py:47
  320.3 0.2 fusion.21
  320.5 8.6 %all_gather.19 = bf16[768,512]{1,0:T(8,128)(2,1)S(1)} all-gather(bf16[768,128]{1,0:T(8,128)(2,1)S(1)} %fusion.21), channel_id=1, replica_groups=mesh['blk'=8,'ch'=4] {'ch'}, dimensions={1}, use_global_device_ids=true | all-gather | bytes 983040 | tf_op jit(solution)/shard_map/all_gather | solution.py:57
  329.1 0.4 fusion.23
  329.5 0.4 fusion.16
  329.9 0.8 copy.14
  (3 shorter events, 0.1 us)
Async XLA Ops:
  6.5 179.4 %copy-start = (bf16[3,512,512]{2,1,0:T(8,128)(2,1)S(1)}, bf16[3,512,512]{2,1,0:T(8,128)(2,1)}, u32[]{:S(2)}) copy-start(bf16[3,512,512]{2,1,0:T(8,128)(2,1)} %param.14) | copy-start | bytes 4718596
  6.5 9.2 %copy-start.2 = (s32[128]{0:T(128)S(1)}, s32[128]{0:T(128)}, u32[]{:S(2)}) copy-start(s32[128]{0:T(128)} %param.12) | copy-start | bytes 1540
  6.5 49.9 %all-gather.3.cloned.1.call-start = ((), (), s32[]{:S(2)}) async-start(), calls=%async_computation | async-start | bytes 1769472 | tf_op jit(solution)/shard_map/all_gather | solution.py:28
  7.3 202.9 %all-gather.5.cloned.1.call-start = ((), (), s32[]{:S(2)}) async-start(), calls=%async_computation.1 | async-start | bytes 1769472 | tf_op jit(solution)/shard_map/all_gather | solution.py:28
  149.5 18.7 %copy-start.1 = (bf16[768,128]{1,0:T(8,128)(2,1)S(1)}, bf16[768,128]{1,0:T(8,128)(2,1)}, u32[]{:S(2)}) copy-start(bf16[768,128]{1,0:T(8,128)(2,1)} %param.9) | copy-start | bytes 589828
Sparse Core Ops, SparseCore 0:
  9.5 46.8 all-gather.2
  167.6 42.5 all-gather.4
where the time goes:
time: 339 us; the launch traced here: 338 us
  local copies, waits for them, and re-layouts  145 us (43%)
  other arithmetic  65.5 us (19%)
  waiting for transfers between devices  64.7 us (19%)
  blocking collectives  26.3 us (8%)
  matrix products  20.9 us (6%)
  between operations  14.9 us (4%)
    gather x2, local copies, waits for them, and re-layouts, cycle_prop(): jnp.take(segment, jnp.clip(row_ids, 0, count_rows - 1).reshape(-1), axis=0)  113 us
    all_gather x2, waiting for transfers between devices, cycle_prop(): segment = lax.all_gather(signal, 'blk', axis=0, tiled=True)  64 us
    scatter-add x2, other arithmetic, cycle_prop(): summed = zero_sum.at[tile_target].add(product)  34 us
    all_gather x3, blocking collectives, mix_term(): lax.all_gather(order_term, 'ch', axis=1, tiled=True)  26.3 us
    select_n x2, other arithmetic, cycle_prop(): jnp.take(segment, jnp.clip(row_ids, 0, count_rows - 1).reshape(-1), axis=0)  23 us
    dot_general x2, matrix products, cycle_prop(): jnp.einsum('gij,gjc->gic', tile_values, picked, preferred_element_type=jn...  19.4 us
    select_n x2, local copies, waits for them, and re-layouts, cycle_prop(): product = jnp.where(in_range[:, None, None], product, 0.0)  18 us
    reshape x2, local copies, waits for them, and re-layouts, cycle_prop(): picked = picked.reshape(window, tile_size, channels)  12.7 us
  transfers between devices with their start and end apart: 2, of which 2 were waited for; matrix products, arithmetic and copies ran while one was open for 3% of the time, Pallas kernels for 0%

commit v1 on v0

--- a/solution.py
+++ b/solution.py
@@ -1,7 +1,342 @@
+import functools
+
 import jax
 import jax.numpy as jnp
 from jax import lax
+from jax.experimental import pallas as pl
+from jax.experimental.pallas import tpu as pltpu
 from jax.sharding import PartitionSpec as P
+
+MESH = pl.DeviceIdType.MESH
+F32 = jnp.float32
+BF16 = jnp.bfloat16
+CHUNK = 16
+
+
+def build_kernel(row_tiles, src, tgt, cnt, tiles_any, a_ref, inv_ref, tiles, sq, pos, sems):
+    block = pl.program_id(0)
+    slots = tiles_any.shape[0]
+    tile = tiles_any.shape[1]
+    chunks = slots // CHUNK
+
+    def fetch(i):
+        return pltpu.make_async_copy(
+            tiles_any.at[pl.ds(i * CHUNK, CHUNK)], tiles.at[pl.ds(i * CHUNK, CHUNK)], sems.at[i]
+        )
+
+    @pl.when(block == 0)
+    def _():
+        for i in range(chunks):
+            fetch(i).start()
+        pos[0] = 0
+        sq[...] = jnp.zeros_like(sq)
+
+    a_ref[...] = jnp.zeros_like(a_ref)
+    live = cnt[0]
+    first = block * row_tiles
+    last = first + row_tiles
+
+    def go(k):
+        return (k < live) & (src[jnp.minimum(k, slots - 1)] < last)
+
+    def body(carry):
+        k, _ = carry
+
+        @pl.when(lax.rem(k, CHUNK) == 0)
+        def _():
+            fetch(lax.div(k, CHUNK)).wait()
+
+        t = tgt[k]
+        rows = pl.ds(pl.multiple_of(t * tile, tile), tile)
+        cols = pl.ds(pl.multiple_of((src[k] - first) * tile, tile), tile)
+        value = tiles[k].astype(F32)
+        a_ref[0, rows, cols] = (a_ref[0, rows, cols].astype(F32) + value).astype(BF16)
+        sq[t] = sq[t] + value * value
+        return k + 1, go(k + 1)
+
+    start = pos[0]
+    end, _ = lax.while_loop(lambda c: c[1], body, (start, go(start)))
+    pos[0] = end
+
+    @pl.when(block == pl.num_programs(0) - 1)
+    def _():
+        for i in range(chunks):
+            @pl.when(i * CHUNK >= end)
+            def _():
+                fetch(i).wait()
+        for t in range(row_tiles):
+            total = jnp.sum(sq[t], axis=1, keepdims=True)
+            inv_ref[pl.ds(t * tile, tile), :] = jnp.broadcast_to(
+                lax.rsqrt(1.0 + total), (tile, tile)
+            )
+
+
+def build(tile_values, tile_source, tile_target, tile_count, row_tiles, blocks):
+    slots, tile, _ = tile_values.shape
+    rows = row_tiles * tile
+    return pl.pallas_call(
+        functools.partial(build_kernel, row_tiles),
+        grid_spec=pltpu.PrefetchScalarGridSpec(
+            num_scalar_prefetch=3,
+            grid=(blocks,),
+            in_specs=[pl.BlockSpec(memory_space=pl.ANY)],
+            out_specs=[
+                pl.BlockSpec((1, rows, rows), lambda b, *_: (b, 0, 0)),
+                pl.BlockSpec((rows, tile), lambda b, *_: (0, 0)),
+            ],
+            scratch_shapes=[
+                pltpu.VMEM((slots, tile, tile), BF16),
+                pltpu.VMEM((row_tiles, tile, tile), F32),
+                pltpu.SMEM((1,), jnp.int32),
+                pltpu.SemaphoreType.DMA((slots // CHUNK,)),
+            ],
+        ),
+        out_shape=[
+            jax.ShapeDtypeStruct((blocks, rows, rows), BF16),
+            jax.ShapeDtypeStruct((rows, tile), F32),
+        ],
+        name="build",
+    )(tile_source, tile_target, tile_count, tile_values)
+
+
+def main_kernel(
+    levels, f_ref, w_any, bias_ref, inv_ref, a_any, out_ref,
+    fall, fld1, fld2, a_v, w_v, acc, base, fw1,
+    asem, wsem, xs, xr, zs1, zr1, ys1, yr1, zs2, zr2, ys2, yr2,
+):
+    rt, tile = f_ref.shape[0], f_ref.shape[1]
+    top = levels - 1
+    me, mc = lax.axis_index("blk"), lax.axis_index("ch")
+    z, y = lax.div(me, 2), lax.rem(me, 2)
+    x, core = lax.div(mc, 2), lax.rem(mc, 2)
+    partner = (me, 2 * x + (1 - core))
+    across = (me, 2 * (1 - x) + core)
+    y_dev = (2 * z + (1 - y), mc)
+    z_dev = ((me + 2, mc), (me - 2, mc))
+    can = (z < top, z > 0)
+
+    for i in range(2 * levels):
+        pltpu.make_async_copy(a_any.at[i], a_v.at[i], asem.at[i]).start()
+    order_of = (mc, partner[1], across[1], 2 * (1 - x) + (1 - core))
+
+    def w_copy(s, o):
+        q = pl.multiple_of(order_of[s] * tile, tile)
+        p = pl.multiple_of(mc * tile, tile)
+        return pltpu.make_async_copy(
+            w_any.at[o, pl.ds(q, tile), pl.ds(p, tile)],
+            w_v.at[s, :, pl.ds(o * tile, tile)],
+            wsem.at[s, o],
+        )
+
+    for s in range(4):
+        for o in range(3):
+            w_copy(s, o).start()
+
+    barrier = pltpu.get_barrier_semaphore()
+    for dev in (partner, across, y_dev):
+        pl.semaphore_signal(barrier, inc=1, device_id=dev, device_id_type=MESH)
+    for d in range(2):
+        @pl.when(can[d])
+        def _():
+            pl.semaphore_signal(barrier, inc=1, device_id=z_dev[d], device_id_type=MESH)
+    pl.semaphore_wait(barrier, 3 + can[0].astype(jnp.int32) + can[1].astype(jnp.int32))
+
+    def remote(src, dst, ssem, rsem, dev):
+        return pltpu.make_async_remote_copy(
+            src_ref=src, dst_ref=dst, send_sem=ssem, recv_sem=rsem, device_id=dev, device_id_type=MESH
+        )
+
+    order = [rt - 1] + list(range(rt - 1))
+
+    def x_copy(kind, c):
+        src = f_ref.at[c] if kind < 2 else fall.at[1, c]
+        return remote(
+            src, fall.at[kind, c], xs.at[kind, c], xr.at[kind, c], across if kind == 1 else partner
+        )
+
+    for c in order:
+        x_copy(1, c).start()
+        x_copy(0, c).start()
+
+    def z_view(fld, d, k, it):
+        level = z - k if d == 0 else z + k
+        return fld.at[2 * level + y, it] if it < rt else fld.at[2 * level + (1 - y), rt - 1]
+
+    def z_copy(fld, zs, zr, d, k, it):
+        view = z_view(fld, d, k, it)
+        return remote(view, view, zs.at[d, k, it], zr.at[d, k, it], z_dev[d])
+
+    def z_has(d, k):
+        return z - k >= 0 if d == 0 else z + k <= top
+
+    def y_index(d, k):
+        return 0 if k == 0 else (1 + k - 1 if d == 0 else levels + k - 1)
+
+    def y_copy(fld, ys, yr, d, k, it):
+        level = z - k if d == 0 else z + k
+        view = fld.at[2 * level + y, it]
+        return remote(view, view, ys.at[y_index(d, k), it], yr.at[y_index(d, k), it], y_dev)
+
+    def y_wait(fld, ys, yr, d, k, it):
+        level = z - k if d == 0 else z + k
+        view = fld.at[2 * level + (1 - y), it]
+        remote(view, view, ys.at[y_index(d, k), it], yr.at[y_index(d, k), it], y_dev).wait_recv()
+
+    def multiply(fld, block, fetch, init=False):
+        if fetch:
+            pltpu.make_async_copy(a_any.at[block], a_v.at[block], asem.at[block]).wait()
+        half = rt * tile // 2
+        rhs = fld[block].reshape(rt * tile, tile)
+
+        @pl.loop(0, 2)
+        def _(h):
+            rows = pl.ds(pl.multiple_of(h * half, half), half)
+            product = jnp.dot(a_v[block, rows, :], rhs, preferred_element_type=F32)
+            acc[rows, :] = product if init else acc[rows, :] + product
+
+    def emit_own(fld, sems, c):
+        zs, zr, ys, yr = sems
+        y_copy(fld, ys, yr, 0, 0, c).start()
+        for d in range(2):
+            @pl.when(can[d])
+            def _():
+                z_copy(fld, zs, zr, d, 0, c).start()
+
+    def gather(fld, sems, fetch):
+        zs, zr, ys, yr = sems
+        y_wait(fld, ys, yr, 0, 0, rt - 1)
+        for d in range(2):
+            @pl.when(can[d])
+            def _():
+                z_copy(fld, zs, zr, d, 0, rt).start()
+        multiply(fld, me, fetch, init=True)
+        for k in range(1, levels):
+            for it in order + [rt]:
+                for d in range(2):
+                    @pl.when(z_has(d, k))
+                    def _():
+                        remote(
+                            z_view(fld, d, k, it), z_view(fld, d, k, it),
+                            zs.at[d, k - 1, it], zr.at[d, k - 1, it], y_dev,
+                        ).wait_recv()
+                        if it < rt - 1:
+                            y_copy(fld, ys, yr, d, k, it).start()
+                        if k < top:
+                            @pl.when(can[d])
+                            def _():
+                                z_copy(fld, zs, zr, d, k, it).start()
+            if k == 1:
+                for it in range(rt - 1):
+                    y_wait(fld, ys, yr, 0, 0, it)
+                multiply(fld, 2 * z + (1 - y), fetch)
+            for d in range(2):
+                @pl.when(z_has(d, k))
+                def _():
+                    level = z - k if d == 0 else z + k
+                    multiply(fld, 2 * level + y, fetch)
+                if k > 1:
+                    other(fld, ys, yr, d, k - 1, fetch)
+        for d in range(2):
+            other(fld, ys, yr, d, top, fetch)
+
+    def other(fld, ys, yr, d, k, fetch):
+        @pl.when(z_has(d, k))
+        def _():
+            for it in range(rt - 1):
+                y_wait(fld, ys, yr, d, k, it)
+            level = z - k if d == 0 else z + k
+            multiply(fld, 2 * level + (1 - y), fetch)
+
+    def drain(fld, sems):
+        zs, zr, ys, yr = sems
+        for it in range(rt):
+            y_copy(fld, ys, yr, 0, 0, it).wait_send()
+        for d in range(2):
+            for k in range(levels):
+                @pl.when(z_has(d, k))
+                def _():
+                    if k > 0:
+                        for it in range(rt - 1):
+                            y_copy(fld, ys, yr, d, k, it).wait_send()
+                    if k < top:
+                        @pl.when(can[d])
+                        def _():
+                            for it in range(rt + 1):
+                                z_copy(fld, zs, zr, d, k, it).wait_send()
+
+    sems1 = (zs1, zr1, ys1, yr1)
+    sems2 = (zs2, zr2, ys2, yr2)
+    bias = bias_ref[:, pl.ds(pl.multiple_of(mc * tile, tile), tile)]
+    for s in range(4):
+        for o in range(3):
+            w_copy(s, o).wait()
+
+    for c in order:
+        x_copy(1, c).wait_recv()
+        x_copy(2, c).start()
+        x_copy(0, c).wait_recv()
+        r = jnp.dot(f_ref[c], w_v[0], preferred_element_type=F32)
+        r += jnp.dot(fall[0, c], w_v[1], preferred_element_type=F32)
+        r += jnp.dot(fall[1, c], w_v[2], preferred_element_type=F32)
+        x_copy(2, c).wait_recv()
+        r += jnp.dot(fall[2, c], w_v[3], preferred_element_type=F32)
+        b2 = r[:, 2 * tile :]
+        fld1[me, c] = b2.astype(BF16)
+        emit_own(fld1, sems1, c)
+        rows = pl.ds(c * tile, tile)
+        base[rows, :] = r[:, :tile] - b2 + bias
+        fw1[rows, :] = r[:, tile : 2 * tile]
+
+    gather(fld1, sems1, True)
+    for c in order:
+        rows = pl.ds(c * tile, tile)
+        fld2[me, c] = (fw1[rows, :] + 2.0 * (acc[rows, :] * inv_ref[rows, :])).astype(BF16)
+        emit_own(fld2, sems2, c)
+    gather(fld2, sems2, False)
+    out_ref[...] = (base[...] + acc[...] * inv_ref[...]).astype(BF16)
+    for kind in range(3):
+        for c in range(rt):
+            x_copy(kind, c).wait_send()
+    drain(fld1, sems1)
+    drain(fld2, sems2)
+
+
+def fast(features, tile_values, tile_source, tile_target, tile_count, weights, bias_vector):
+    tile = tile_values.shape[1]
+    rows, cols = features.shape
+    rt = rows // tile
+    blocks = lax.axis_size("blk")
+    levels = blocks // 2
+    a, inv = build(tile_values, tile_source, tile_target, tile_count, rt, blocks)
+    vmem = pl.BlockSpec(memory_space=pltpu.VMEM)
+    hbm = pl.BlockSpec(memory_space=pl.ANY)
+    dma = pltpu.SemaphoreType.DMA
+    gather_sems = [
+        dma((2, levels - 1, rt + 1)), dma((2, levels - 1, rt + 1)),
+        dma((2 * levels - 1, rt)), dma((2 * levels - 1, rt)),
+    ]
+    return pl.pallas_call(
+        functools.partial(main_kernel, levels),
+        out_shape=jax.ShapeDtypeStruct((rows, cols), BF16),
+        in_specs=[vmem, hbm, vmem, vmem, hbm],
+        out_specs=vmem,
+        scratch_shapes=[
+            pltpu.VMEM((3, rt, tile, tile), BF16),
+            pltpu.VMEM((blocks, rt, tile, tile), BF16),
+            pltpu.VMEM((blocks, rt, tile, tile), BF16),
+            pltpu.VMEM((blocks, rows, rows), BF16),
+            pltpu.VMEM((4, tile, 3 * tile), BF16),
+            pltpu.VMEM((rows, tile), F32),
+            pltpu.VMEM((rows, tile), F32),
+            pltpu.VMEM((rows, tile), F32),
+            dma((blocks,)),
+            dma((4, 3)),
+            dma((3, rt)),
+            dma((3, rt)),
+        ] + gather_sems + gather_sems,
+        compiler_params=pltpu.CompilerParams(collective_id=0, has_side_effects=True),
+        name="propagate",
+    )(features.reshape(rt, tile, cols), weights, bias_vector.reshape(1, -1), inv, a)
 
 
 def per_device(features, tile_values, tile_source, tile_target, tile_count, weights, bias_vector):
@@ -70,8 +405,9 @@
 
 
 def solution(mesh):
+    dense = mesh.shape["blk"] == 8 and mesh.shape["ch"] == 4
     return jax.shard_map(
-        per_device,
+        fast if dense else per_device,
         mesh=mesh,
         in_specs=(P("blk", "ch"), P("blk", None, None), P("blk"), P("blk"), P("blk"), P(), P()),
         out_specs=P("blk", "ch"),

time: 339 us -> 64.2 us (0.19)
  local copies, waits for them, and re-layouts: 145 us -> 1.62 us
  other arithmetic: 65.5 us -> 0 us
  waiting for transfers between devices: 64.7 us -> 0 us
  Pallas kernels: 0 us -> 61.8 us
  blocking collectives: 26.3 us -> 0 us
  matrix products: 20.9 us -> 0 us
  between operations: 14.9 us -> 0.67 us
    gather x2 -> x0, local copies, waits for them, and re-layouts: 113 us -> none  [cycle_prop(): jnp.take(segment, jnp.clip(row_ids, 0, count_rows - 1).reshape(-1), axis=0)]
    all_gather x2 -> x0, waiting for transfers between devices: 64 us -> none  [cycle_prop(): segment = lax.all_gather(signal, 'blk', axis=0, tiled=True)]
    pallas_call x0 -> x2, Pallas kernels: none -> 61.8 us  [the longest x1 53 us: fast(): pl.pallas_call(functools.partial(main_kernel, levels), out_shape=jax.Shap...]
    scatter-add x2 -> x0, other arithmetic: 34 us -> none  [cycle_prop(): summed = zero_sum.at[tile_target].add(product)]
    all_gather x3 -> x0, blocking collectives: 26.3 us -> none  [mix_term(): lax.all_gather(order_term, 'ch', axis=1, tiled=True)]
    select_n x2 -> x0, other arithmetic: 23 us -> none  [cycle_prop(): jnp.take(segment, jnp.clip(row_ids, 0, count_rows - 1).reshape(-1), axis=0)]
    dot_general x6 -> x0, matrix products: 20.9 us -> none  [the longest x2 19.4 us: cycle_prop(): jnp.einsum('gij,gjc->gic', tile_values, picked, preferred_element_type=jn...]
    select_n x2 -> x0, local copies, waits for them, and re-layouts: 18 us -> none  [cycle_prop(): product = jnp.where(in_range[:, None, None], product, 0.0)]
  transfers between devices with their start and end apart: 2 -> 0, of which waited for: 2 -> 0; matrix products, arithmetic and copies ran while one was open for 3% -> 0% of each run, Pallas kernels for 0% -> 0%
where the time goes in v1:
time: 64.2 us; the launch traced here: 64 us
  Pallas kernels  61.8 us (96%)
  local copies, waits for them, and re-layouts  1.62 us (3%)
  between operations  0.67 us (1%)
    pallas_call x1, Pallas kernels, fast(): pl.pallas_call(functools.partial(main_kernel, levels), out_shape=jax.Shap...  53 us
    pallas_call x1, Pallas kernels, build(): pl.pallas_call(functools.partial(build_kernel, row_tiles), grid_spec=pltp...  8.73 us
    unnamed x1, local copies, waits for them, and re-layouts  1.62 us

profile of v1, /device:TPU:0, one launch (start us, length us, event | category | flops | bytes accessed | tf_op | source)
XLA Modules:
  0.0 64.0 jit_solution(17651815344518543170)
XLA Ops:
  0.7 8.7 %build.1 = (bf16[8,768,768]{2,1,0:T(8,128)(2,1)}, f32[768,128]{1,0:T(8,128)}) custom-call(s32[128]{0:T(128)} %src.1, s32[128]{0:T(128)} %tgt.1, s32[1]{0:T(128)S(6)} %copy.9.cnt, bf16[128,128,128]{2,1,0:T(8,128)(2,1)} %tiles_any.1), custom_call_target="tpu_custom_call" | custom-call | tf_op jit(solution)/shard_map/build/pallas_call | solution.py:77
  9.4 53.0 %propagate.1 = bf16[768,128]{1,0:T(8,128)(2,1)} custom-call(bf16[6,128,128]{2,1,0:T(8,128)(2,1)} %bitcast.2, bf16[3,512,512]{2,1,0:T(8,128)(2,1)} %w_any.1, f32[1,512]{1,0:T(1,128)} %bitcast.3, f32[768,128]{1,0:T(8,128)} %get-tuple-element.7.inv_ref, bf16[8,768,768]{2,1,0:T(8,128)(2,1)} %get-tuple-element.8.a_any), custom_call_target="tpu_custom_call" | custom-call | tf_op jit(solution)/shard_map/propagate/pallas_call | solution.py:318
  62.4 1.6 %copy.10 = bf16[768,128]{1,0:T(8,128)(2,1)} copy(bf16[768,128]{1,0:T(8,128)(2,1)} %propagate.1) | data formatting | bytes 393216

commit v2 on v1

--- a/solution.py
+++ b/solution.py
@@ -10,101 +10,105 @@
 MESH = pl.DeviceIdType.MESH
 F32 = jnp.float32
 BF16 = jnp.bfloat16
-CHUNK = 16
-
-
-def build_kernel(row_tiles, src, tgt, cnt, tiles_any, a_ref, inv_ref, tiles, sq, pos, sems):
-    block = pl.program_id(0)
+
+
+def merge_kernel(
+    row_tiles, src, tgt, cnt, tiles_any, idx, extra_any, got, total, packed, slot_group, insem, outsem
+):
     slots = tiles_any.shape[0]
-    tile = tiles_any.shape[1]
-    chunks = slots // CHUNK
-
-    def fetch(i):
-        return pltpu.make_async_copy(
-            tiles_any.at[pl.ds(i * CHUNK, CHUNK)], tiles.at[pl.ds(i * CHUNK, CHUNK)], sems.at[i]
-        )
-
-    @pl.when(block == 0)
-    def _():
-        for i in range(chunks):
-            fetch(i).start()
-        pos[0] = 0
-        sq[...] = jnp.zeros_like(sq)
-
-    a_ref[...] = jnp.zeros_like(a_ref)
-    live = cnt[0]
-    first = block * row_tiles
-    last = first + row_tiles
-
-    def go(k):
-        return (k < live) & (src[jnp.minimum(k, slots - 1)] < last)
-
-    def body(carry):
-        k, _ = carry
-
-        @pl.when(lax.rem(k, CHUNK) == 0)
+    empty = slots + extra_any.shape[0]
+
+    @pl.loop(0, idx.shape[0] // 8)
+    def _(p):
+        for q in range(8):
+            idx[p * 8 + q] = empty
+
+    def fetch(slot, entry):
+        return pltpu.make_async_copy(tiles_any.at[slot], got.at[entry], insem.at[entry])
+
+    def scan(k, carry):
+        place = src[k] * row_tiles + tgt[k]
+        held = idx[place]
+        groups, entries = carry
+
+        @pl.when(held == empty)
         def _():
-            fetch(lax.div(k, CHUNK)).wait()
-
-        t = tgt[k]
-        rows = pl.ds(pl.multiple_of(t * tile, tile), tile)
-        cols = pl.ds(pl.multiple_of((src[k] - first) * tile, tile), tile)
-        value = tiles[k].astype(F32)
-        a_ref[0, rows, cols] = (a_ref[0, rows, cols].astype(F32) + value).astype(BF16)
-        sq[t] = sq[t] + value * value
-        return k + 1, go(k + 1)
-
-    start = pos[0]
-    end, _ = lax.while_loop(lambda c: c[1], body, (start, go(start)))
-    pos[0] = end
-
-    @pl.when(block == pl.num_programs(0) - 1)
-    def _():
-        for i in range(chunks):
-            @pl.when(i * CHUNK >= end)
-            def _():
-                fetch(i).wait()
-        for t in range(row_tiles):
-            total = jnp.sum(sq[t], axis=1, keepdims=True)
-            inv_ref[pl.ds(t * tile, tile), :] = jnp.broadcast_to(
-                lax.rsqrt(1.0 + total), (tile, tile)
-            )
-
-
-def build(tile_values, tile_source, tile_target, tile_count, row_tiles, blocks):
+            idx[place] = k
+
+        fresh = held < slots
+        again = held < empty
+
+        @pl.when(fresh)
+        def _():
+            idx[place] = slots + groups
+            fetch(held, entries).start()
+            slot_group[entries] = groups
+
+        step = fresh.astype(jnp.int32)
+
+        @pl.when(again)
+        def _():
+            fetch(k, entries + step).start()
+            slot_group[entries + step] = jnp.where(fresh, groups, held - slots)
+
+        return groups + step, entries + step + again.astype(jnp.int32)
+
+    groups, entries = lax.fori_loop(0, cnt[0], scan, (jnp.int32(0), jnp.int32(0)))
+
+    @pl.loop(0, groups)
+    def _(g):
+        total[g] = jnp.zeros_like(total[g])
+
+    @pl.loop(0, entries)
+    def _(e):
+        fetch(0, e).wait()
+        g = slot_group[e]
+        total[g] = total[g] + got[e].astype(F32)
+
+    def put(g):
+        return pltpu.make_async_copy(packed.at[g], extra_any.at[g], outsem.at[g])
+
+    @pl.loop(0, groups)
+    def _(g):
+        packed[g] = total[g].astype(BF16)
+        put(g).start()
+
+    @pl.loop(0, groups)
+    def _(g):
+        put(g).wait()
+
+
+def merge(tile_values, tile_source, tile_target, tile_count, row_tiles, blocks):
     slots, tile, _ = tile_values.shape
-    rows = row_tiles * tile
+    smem = pl.BlockSpec(memory_space=pltpu.SMEM)
+    hbm = pl.BlockSpec(memory_space=pl.ANY)
+    groups = slots // 2
     return pl.pallas_call(
-        functools.partial(build_kernel, row_tiles),
-        grid_spec=pltpu.PrefetchScalarGridSpec(
-            num_scalar_prefetch=3,
-            grid=(blocks,),
-            in_specs=[pl.BlockSpec(memory_space=pl.ANY)],
-            out_specs=[
-                pl.BlockSpec((1, rows, rows), lambda b, *_: (b, 0, 0)),
-                pl.BlockSpec((rows, tile), lambda b, *_: (0, 0)),
-            ],
-            scratch_shapes=[
-                pltpu.VMEM((slots, tile, tile), BF16),
-                pltpu.VMEM((row_tiles, tile, tile), F32),
-                pltpu.SMEM((1,), jnp.int32),
-                pltpu.SemaphoreType.DMA((slots // CHUNK,)),
-            ],
-        ),
+        functools.partial(merge_kernel, row_tiles),
+        in_specs=[smem, smem, smem, hbm],
+        out_specs=[smem, hbm],
+        scratch_shapes=[
+            pltpu.VMEM((slots, tile, tile), BF16),
+            pltpu.VMEM((groups, tile, tile), F32),
+            pltpu.VMEM((groups, tile, tile), BF16),
+            pltpu.SMEM((slots,), jnp.int32),
+            pltpu.SemaphoreType.DMA((slots,)),
+            pltpu.SemaphoreType.DMA((groups,)),
+        ],
         out_shape=[
-            jax.ShapeDtypeStruct((blocks, rows, rows), BF16),
-            jax.ShapeDtypeStruct((rows, tile), F32),
+            jax.ShapeDtypeStruct((blocks * row_tiles * row_tiles,), jnp.int32),
+            jax.ShapeDtypeStruct((groups, tile, tile), BF16),
         ],
-        name="build",
+        name="merge",
     )(tile_source, tile_target, tile_count, tile_values)
 
 
 def main_kernel(
-    levels, f_ref, w_any, bias_ref, inv_ref, a_any, out_ref,
-    fall, fld1, fld2, a_v, w_v, acc, base, fw1,
-    asem, wsem, xs, xr, zs1, zr1, ys1, yr1, zs2, zr2, ys2, yr2,
+    levels, f_any, w_any, bias_ref, tgt, cnt, idx, tiles_any, extra_any, out_ref,
+    f_ref, fall, fld1, fld2, a_v, tiles, w_v, acc, base, fw1, inv_ref,
+    fsem, asem, wsem, xs, xr, zs1, zr1, ys1, yr1, zs2, zr2, ys2, yr2,
 ):
-    rt, tile = f_ref.shape[0], f_ref.shape[1]
+    rt, tile = f_any.shape[0], f_any.shape[1]
     top = levels - 1
     me, mc = lax.axis_index("blk"), lax.axis_index("ch")
     z, y = lax.div(me, 2), lax.rem(me, 2)
@@ -115,8 +119,21 @@
     z_dev = ((me + 2, mc), (me - 2, mc))
     can = (z < top, z > 0)
 
-    for i in range(2 * levels):
-        pltpu.make_async_copy(a_any.at[i], a_v.at[i], asem.at[i]).start()
+    barrier = pltpu.get_barrier_semaphore()
+    for dev in (partner, across, y_dev):
+        pl.semaphore_signal(barrier, inc=1, device_id=dev, device_id_type=MESH)
+    for d in range(2):
+        @pl.when(can[d])
+        def _():
+            pl.semaphore_signal(barrier, inc=1, device_id=z_dev[d], device_id_type=MESH)
+
+    slots, extras = tiles_any.shape[0], extra_any.shape[0]
+
+    def f_copy(c):
+        return pltpu.make_async_copy(f_any.at[c], f_ref.at[c], fsem.at[c])
+
+    for c in [rt - 1] + list(range(rt - 1)):
+        f_copy(c).start()
     order_of = (mc, partner[1], across[1], 2 * (1 - x) + (1 - core))
 
     def w_copy(s, o):
@@ -132,13 +149,6 @@
         for o in range(3):
             w_copy(s, o).start()
 
-    barrier = pltpu.get_barrier_semaphore()
-    for dev in (partner, across, y_dev):
-        pl.semaphore_signal(barrier, inc=1, device_id=dev, device_id_type=MESH)
-    for d in range(2):
-        @pl.when(can[d])
-        def _():
-            pl.semaphore_signal(barrier, inc=1, device_id=z_dev[d], device_id_type=MESH)
     pl.semaphore_wait(barrier, 3 + can[0].astype(jnp.int32) + can[1].astype(jnp.int32))
 
     def remote(src, dst, ssem, rsem, dev):
@@ -149,7 +159,7 @@
     order = [rt - 1] + list(range(rt - 1))
 
     def x_copy(kind, c):
-        src = f_ref.at[c] if kind < 2 else fall.at[1, c]
+        src = f_any.at[c] if kind < 2 else fall.at[1, c]
         return remote(
             src, fall.at[kind, c], xs.at[kind, c], xr.at[kind, c], across if kind == 1 else partner
         )
@@ -157,6 +167,13 @@
     for c in order:
         x_copy(1, c).start()
         x_copy(0, c).start()
+    tile_copies = (
+        pltpu.make_async_copy(tiles_any, tiles.at[pl.ds(0, slots)], asem.at[0]),
+        pltpu.make_async_copy(extra_any, tiles.at[pl.ds(slots, extras)], asem.at[1]),
+    )
+    for copy in tile_copies:
+        copy.start()
+    tiles[slots + extras] = jnp.zeros((tile, tile), BF16)
 
     def z_view(fld, d, k, it):
         level = z - k if d == 0 else z + k
@@ -182,9 +199,36 @@
         view = fld.at[2 * level + (1 - y), it]
         remote(view, view, ys.at[y_index(d, k), it], yr.at[y_index(d, k), it], y_dev).wait_recv()
 
+    def fill(block):
+        @pl.loop(0, rt)
+        def _(t):
+            for j in range(rt):
+                a_v[block, pl.ds(pl.multiple_of(t * tile, tile), tile), pl.ds(j * tile, tile)] = (
+                    tiles[idx[(block * rt + j) * rt + t]]
+                )
+
+    def norms():
+        part = 32
+        for r in range(tile // part):
+            def add(k, sums):
+                value = tiles[k, pl.ds(r * part, part), :].astype(F32)
+                value = value * value
+                aim = jnp.where(k < cnt[0], tgt[k], rt)
+                return tuple(
+                    sums[t] + value * jnp.where(aim == t, 1.0, 0.0).astype(F32) for t in range(rt)
+                )
+
+            zero = jnp.zeros((part, tile), F32)
+            sums = lax.fori_loop(0, slots, add, (zero,) * rt)
+            for t in range(rt):
+                total = jnp.sum(sums[t], axis=1, keepdims=True)
+                inv_ref[pl.ds(t * tile + r * part, part), :] = jnp.broadcast_to(
+                    lax.rsqrt(1.0 + total), (part, tile)
+                )
+
     def multiply(fld, block, fetch, init=False):
         if fetch:
-            pltpu.make_async_copy(a_any.at[block], a_v.at[block], asem.at[block]).wait()
+            fill(block)
         half = rt * tile // 2
         rhs = fld[block].reshape(rt * tile, tile)
 
@@ -209,6 +253,10 @@
             @pl.when(can[d])
             def _():
                 z_copy(fld, zs, zr, d, 0, rt).start()
+        if fetch:
+            for copy in tile_copies:
+                copy.wait()
+            norms()
         multiply(fld, me, fetch, init=True)
         for k in range(1, levels):
             for it in order + [rt]:
@@ -274,6 +322,7 @@
     for c in order:
         x_copy(1, c).wait_recv()
         x_copy(2, c).start()
+        f_copy(c).wait()
         x_copy(0, c).wait_recv()
         r = jnp.dot(f_ref[c], w_v[0], preferred_element_type=F32)
         r += jnp.dot(fall[0, c], w_v[1], preferred_element_type=F32)
@@ -307,9 +356,11 @@
     rt = rows // tile
     blocks = lax.axis_size("blk")
     levels = blocks // 2
-    a, inv = build(tile_values, tile_source, tile_target, tile_count, rt, blocks)
+    idx, extra = merge(tile_values, tile_source, tile_target, tile_count, rt, blocks)
     vmem = pl.BlockSpec(memory_space=pltpu.VMEM)
     hbm = pl.BlockSpec(memory_space=pl.ANY)
+    smem = pl.BlockSpec(memory_space=pltpu.SMEM)
+    slots = tile_values.shape[0]
     dma = pltpu.SemaphoreType.DMA
     gather_sems = [
         dma((2, levels - 1, rt + 1)), dma((2, levels - 1, rt + 1)),
@@ -318,25 +369,30 @@
     return pl.pallas_call(
         functools.partial(main_kernel, levels),
         out_shape=jax.ShapeDtypeStruct((rows, cols), BF16),
-        in_specs=[vmem, hbm, vmem, vmem, hbm],
+        in_specs=[hbm, hbm, vmem, smem, smem, smem, hbm, hbm],
         out_specs=vmem,
         scratch_shapes=[
+            pltpu.VMEM((rt, tile, tile), BF16),
             pltpu.VMEM((3, rt, tile, tile), BF16),
             pltpu.VMEM((blocks, rt, tile, tile), BF16),
             pltpu.VMEM((blocks, rt, tile, tile), BF16),
             pltpu.VMEM((blocks, rows, rows), BF16),
+            pltpu.VMEM((slots + slots // 2 + 1, tile, tile), BF16),
             pltpu.VMEM((4, tile, 3 * tile), BF16),
             pltpu.VMEM((rows, tile), F32),
             pltpu.VMEM((rows, tile), F32),
             pltpu.VMEM((rows, tile), F32),
-            dma((blocks,)),
+            pltpu.VMEM((rows, tile), F32),
+            dma((rt,)),
+            dma((2,)),
             dma((4, 3)),
             dma((3, rt)),
             dma((3, rt)),
         ] + gather_sems + gather_sems,
         compiler_params=pltpu.CompilerParams(collective_id=0, has_side_effects=True),
         name="propagate",
-    )(features.reshape(rt, tile, cols), weights, bias_vector.reshape(1, -1), inv, a)
+    )(features.reshape(rt, tile, cols), weights, bias_vector.reshape(1, -1),
+      tile_target, tile_count, idx, tile_values, extra)
 
 
 def per_device(features, tile_values, tile_source, tile_target, tile_count, weights, bias_vector):

time: 64.2 us -> 72.8 us (1.13)
  Pallas kernels: 61.8 us -> 69.7 us
    pallas_call x1, Pallas kernels: 53 us -> 63.8 us  [fast(): pl.pallas_call(functools.partial(main_kernel, levels), out_shape=jax.Shap...]
    pallas_call x1, Pallas kernels: 8.73 us -> 5.93 us  [merge(): pl.pallas_call(functools.partial(merge_kernel, row_tiles), in_specs=[smem...]
where the time goes in v2:
time: 72.8 us; the launch traced here: 72 us
  Pallas kernels  69.7 us (96%)
  local copies, waits for them, and re-layouts  1.62 us (2%)
    pallas_call x1, Pallas kernels, fast(): pl.pallas_call(functools.partial(main_kernel, levels), out_shape=jax.Shap...  63.8 us
    pallas_call x1, Pallas kernels, merge(): pl.pallas_call(functools.partial(merge_kernel, row_tiles), in_specs=[smem...  5.93 us
    unnamed x1, local copies, waits for them, and re-layouts  1.62 us

profile of v2, /device:TPU:0, one launch (start us, length us, event | category | flops | bytes accessed | tf_op | source)
XLA Modules:
  0.0 72.0 jit_solution(12767133271365482677)
XLA Ops:
  0.7 5.9 %merge.1 = (s32[288]{0:T(512)}, bf16[64,128,128]{2,1,0:T(8,128)(2,1)}) custom-call(s32[128]{0:T(128)} %src.1, s32[128]{0:T(128)} %tgt.3, s32[1]{0:T(128)S(6)} %copy.9.cnt, bf16[128,128,128]{2,1,0:T(8,128)(2,1)} %tiles_any.3), custom_call_target="tpu_custom_call" | custom-call | tf_op jit(solution)/shard_map/merge/pallas_call | solution.py:86
  6.6 63.8 %propagate.1 = bf16[768,128]{1,0:T(8,128)(2,1)} custom-call(bf16[6,128,128]{2,1,0:T(8,128)(2,1)} %bitcast.2, bf16[3,512,512]{2,1,0:T(8,128)(2,1)} %w_any.1, f32[1,512]{1,0:T(1,128)} %bitcast.3, s32[128]{0:T(128)} %tgt.3, s32[1]{0:T(128)S(6)} %copy.9.cnt, s32[288]{0:T(512)} %get-tuple-element.7.idx, bf16[128,128,128]{2,1,0:T(8,128)(2,1)} %tiles_any.3, ...), custom_call_target="tpu_custom_call" | custom-call | tf_op jit(solution)/shard_map/propagate/pallas_call | solution.py:369
  70.4 1.6 %copy.10 = bf16[768,128]{1,0:T(8,128)(2,1)} copy(bf16[768,128]{1,0:T(8,128)(2,1)} %propagate.1) | data formatting | bytes 393216

commit v3 on v1

--- a/solution.py
+++ b/solution.py
@@ -79,7 +79,7 @@
         grid_spec=pltpu.PrefetchScalarGridSpec(
             num_scalar_prefetch=3,
             grid=(blocks,),
-            in_specs=[pl.BlockSpec(memory_space=pl.ANY)],
+            in_specs=[pl.BlockSpec(memory_space=pltpu.HBM)],
             out_specs=[
                 pl.BlockSpec((1, rows, rows), lambda b, *_: (b, 0, 0)),
                 pl.BlockSpec((rows, tile), lambda b, *_: (0, 0)),
@@ -95,6 +95,7 @@
             jax.ShapeDtypeStruct((blocks, rows, rows), BF16),
             jax.ShapeDtypeStruct((rows, tile), F32),
         ],
+        compiler_params=pltpu.CompilerParams(vmem_limit_bytes=24 << 20),
         name="build",
     )(tile_source, tile_target, tile_count, tile_values)
 
@@ -309,7 +310,7 @@
     levels = blocks // 2
     a, inv = build(tile_values, tile_source, tile_target, tile_count, rt, blocks)
     vmem = pl.BlockSpec(memory_space=pltpu.VMEM)
-    hbm = pl.BlockSpec(memory_space=pl.ANY)
+    hbm = pl.BlockSpec(memory_space=pltpu.HBM)
     dma = pltpu.SemaphoreType.DMA
     gather_sems = [
         dma((2, levels - 1, rt + 1)), dma((2, levels - 1, rt + 1)),
@@ -334,7 +335,7 @@
             dma((3, rt)),
             dma((3, rt)),
         ] + gather_sems + gather_sems,
-        compiler_params=pltpu.CompilerParams(collective_id=0, has_side_effects=True),
+        compiler_params=pltpu.CompilerParams(collective_id=0, has_side_effects=True, vmem_limit_bytes=32 << 20),
         name="propagate",
     )(features.reshape(rt, tile, cols), weights, bias_vector.reshape(1, -1), inv, a)
 

time: 64.2 us -> 63.1 us (0.983)
  Pallas kernels: 61.8 us -> 58 us
  local copies, waits for them, and re-layouts: 1.62 us -> 4.18 us
    pallas_call x1, Pallas kernels: 8.73 us -> 3.31 us  [build(): pl.pallas_call(functools.partial(build_kernel, row_tiles), grid_spec=pltp...]
    unnamed x1 -> x13, local copies, waits for them, and re-layouts: 1.62 us -> 4.18 us
    pallas_call x1, Pallas kernels: 53 us -> 54.6 us  [fast(): pl.pallas_call(functools.partial(main_kernel, levels), out_shape=jax.Shap...]
where the time goes in v3:
time: 63.1 us; the launch traced here: 62.9 us
  Pallas kernels  58 us (92%)
  local copies, waits for them, and re-layouts  4.18 us (7%)
  between operations  0.72 us (1%)
    pallas_call x1, Pallas kernels, fast(): pl.pallas_call(functools.partial(main_kernel, levels), out_shape=jax.Shap...  54.6 us
    unnamed x13, local copies, waits for them, and re-layouts  4.18 us
    pallas_call x1, Pallas kernels, build(): pl.pallas_call(functools.partial(build_kernel, row_tiles), grid_spec=pltp...  3.31 us

profile of v3, /device:TPU:0, one launch (start us, length us, event | category | flops | bytes accessed | tf_op | source)
XLA Modules:
  0.0 62.9 jit_solution(3640876680964839418)
XLA Ops:
  0.0 0.0 copy-start.3
  0.7 0.0 copy-start
  0.7 2.2 %copy-done = bf16[128,128,128]{2,1,0:T(8,128)(2,1)S(1)} copy-done((bf16[128,128,128]{2,1,0:T(8,128)(2,1)S(1)}, bf16[128,128,128]{2,1,0:T(8,128)(2,1)}, u32[]{:S(2)}) %copy-start) | copy-done | bytes 4194328
  2.9 0.0 copy-start.4
  2.9 0.7 %copy-done.4 = s32[128]{0:T(128)S(1)} copy-done((s32[128]{0:T(128)S(1)}, s32[128]{0:T(128)}, u32[]{:S(2)}) %copy-start.4) | copy-done | bytes 536
  3.5 0.0 copy-start.5
  3.5 0.7 %copy-done.5 = s32[128]{0:T(128)S(1)} copy-done((s32[128]{0:T(128)S(1)}, s32[128]{0:T(128)}, u32[]{:S(2)}) %copy-start.5) | copy-done | bytes 536
  4.2 0.0 copy-start.1
  4.2 0.0 copy-start.2
  4.2 3.3 %build.1 = (bf16[8,768,768]{2,1,0:T(8,128)(2,1)S(1)}, f32[768,128]{1,0:T(8,128)S(1)}) custom-call(s32[128]{0:T(128)S(1)} %copy-done.4, s32[128]{0:T(128)S(1)} %copy-done.5, s32[1]{0:T(128)S(6)} %copy.9.cnt, bf16[128,128,128]{2,1,0:T(8,128)(2,1)S(1)} %copy-done), custom_call_target="tpu_custom_call" | custom-call | tf_op jit(solution)/shard_map/build/pallas_call | solution.py:77
  7.5 0.0 copy-done.3
  7.5 0.0 copy-done.1
  7.5 0.0 copy-done.2
  7.5 54.6 %propagate.1 = bf16[768,128]{1,0:T(8,128)(2,1)S(1)} custom-call(bf16[6,128,128]{2,1,0:T(8,128)(2,1)S(1)} %bitcast.2, bf16[3,512,512]{2,1,0:T(8,128)(2,1)S(1)} %copy-done.1, f32[1,512]{1,0:T(1,128)S(1)} %bitcast.3, f32[768,128]{1,0:T(8,128)S(1)} %get-tuple-element.7.inv_ref, bf16[8,768,768]{2,1,0:T(8,128)(2,1)S(1)} %get-tuple-element.8.a_any), custom_call_target="tpu_custom_call" | custom-call | tf_op jit(solution)/shard_map/propagate/pallas_call | solution.py:319
  62.2 0.7 %copy.10 = bf16[768,128]{1,0:T(8,128)(2,1)} copy(bf16[768,128]{1,0:T(8,128)(2,1)S(1)} %propagate.1) | data formatting | bytes 393216
Async XLA Ops:
  0.0 7.5 %copy-start.3 = (f32[512]{0:T(512)S(1)}, f32[512]{0:T(512)}, u32[]{:S(2)}) copy-start(f32[512]{0:T(512)} %param.13) | copy-start | bytes 6148
  0.7 2.2 %copy-start = (bf16[128,128,128]{2,1,0:T(8,128)(2,1)S(1)}, bf16[128,128,128]{2,1,0:T(8,128)(2,1)}, u32[]{:S(2)}) copy-start(bf16[128,128,128]{2,1,0:T(8,128)(2,1)} %tiles_any.1) | copy-start | bytes 12582916
  2.9 0.7 %copy-start.4 = (s32[128]{0:T(128)S(1)}, s32[128]{0:T(128)}, u32[]{:S(2)}) copy-start(s32[128]{0:T(128)} %src.1) | copy-start | bytes 1540
  3.5 0.7 %copy-start.5 = (s32[128]{0:T(128)S(1)}, s32[128]{0:T(128)}, u32[]{:S(2)}) copy-start(s32[128]{0:T(128)} %tgt.1) | copy-start | bytes 1540
  4.2 3.3 %copy-start.1 = (bf16[3,512,512]{2,1,0:T(8,128)(2,1)S(1)}, bf16[3,512,512]{2,1,0:T(8,128)(2,1)}, u32[]{:S(2)}) copy-start(bf16[3,512,512]{2,1,0:T(8,128)(2,1)} %w_any.1) | copy-start | bytes 4718596
  4.2 3.3 %copy-start.2 = (bf16[768,128]{1,0:T(8,128)(2,1)S(1)}, bf16[768,128]{1,0:T(8,128)(2,1)}, u32[]{:S(2)}) copy-start(bf16[768,128]{1,0:T(8,128)(2,1)} %param.7) | copy-start | bytes 589828
